TPU v7x, 128 devices: a whole 4x4x4 slice. The times are simulated.
128 devices in a mesh: dom: 8 (over y, core), grp: 16 (over z, x).
Axes of the slice: x: 4, y: 4, z: 4, core: 2. Of those that a mesh axis runs over, the one named last changes fastest.
Arguments:
- basis_values: bfloat16 [14336, 320, 256], P(('dom', 'grp')), may hold values from -0.47851562 to 0.47851562
- point_weights: float32 [14336, 256], P(('dom', 'grp')), may hold values from -6 to 6
- batch_blocks: int32 [14336, 5], P(('dom', 'grp')), may hold values from 0 to 31, as said below
- live_count: int32 [8, 16], P('dom', 'grp'), may hold values from 28 to 112, as said below
- dom_blocks: int32 [8, 32], replicated, may hold values from 0 to 255, as said below
- pair_mask: int32 [8, 32, 32], P('dom'), may hold values 0 or 1
Outputs:
- hamiltonian: float32 [16384, 16384], P('dom', 'grp')
Inputs may be any that keep to these rules, and one draw needn't show every extreme that they name: `batch_blocks`: each batch names 5 different domain-local blocks. `dom_blocks`: the 32 blocks of a domain are different, and block p's global number is congruent to p modulo 16. Neighbouring domains share some blocks. `live_count`: some device holds 112 live batches in every draw, and some holds 28.
All inputs are finite; a program needn't handle non-finite values. No bound on the sum of `pair_mask` on one device may be relied on, other than what follows from the above.
Results may differ from a plain program's by a relative error of at most 0.0029.
Values sent between devices are 32-bit elements; how exact they have to be, the bound alone decides.
A program may use at most 128 MiB of HBM per device.

v0:
```python
import jax
import jax.numpy as jnp
from jax import lax
from jax.sharding import PartitionSpec as P

BLK = 64
NBLK = 256
NBT = 5
KB = 32


def local(basis_values, point_weights, batch_blocks, live_count, dom_blocks, pair_mask):
    dom_count = lax.axis_size("dom")
    grp_count = lax.axis_size("grp")
    my_dom = lax.axis_index("dom")
    my_grp = lax.axis_index("grp")
    row_slots = KB // dom_count
    col_slots = KB // grp_count
    tile_size = BLK * BLK
    group_size = 8
    batch_slots = basis_values.shape[0]
    live_here = live_count[0, 0]

    def place_of(row_block, col_block):
        return (
            (row_block % dom_count * grp_count + col_block % grp_count) * row_slots
            + row_block // dom_count
        ) * col_slots + col_block // grp_count

    def accumulate(number, partial_value):
        start = (number * group_size).astype(jnp.int32)
        values = lax.dynamic_slice_in_dim(basis_values, start, group_size, 0)
        weights = lax.dynamic_slice_in_dim(point_weights, start, group_size, 0)
        slot_ids = start + jnp.arange(group_size, dtype=jnp.int32)
        weights = jnp.where((slot_ids < live_here)[:, None], weights, jnp.zeros_like(weights))
        scaled = (values.astype(jnp.float32) * weights[:, None, :]).astype(jnp.bfloat16)
        product = jnp.einsum("bfp,bgp->bfg", values, scaled, preferred_element_type=jnp.float32)
        tiles = (
            product.reshape(group_size, NBT, BLK, NBT, BLK)
            .transpose(0, 1, 3, 2, 4)
            .reshape(group_size * NBT * NBT, tile_size)
        )
        blocks = lax.dynamic_slice_in_dim(batch_blocks, start, group_size, 0)
        targets = place_of(blocks[:, :, None], blocks[:, None, :]).reshape(-1)
        return partial_value.at[targets].add(tiles)

    partial_value = lax.fori_loop(
        0, batch_slots // group_size, accumulate, jnp.zeros((KB * KB, tile_size), jnp.float32)
    )
    mask_local = (
        pair_mask[0]
        .reshape(row_slots, dom_count, col_slots, grp_count)
        .transpose(1, 3, 0, 2)
        .reshape(-1)
    )
    partial_value = partial_value * mask_local[:, None].astype(jnp.float32)
    partial_value = partial_value.reshape(dom_count, grp_count, row_slots * col_slots, tile_size)
    summed = lax.psum(partial_value, "grp")
    own_share = lax.dynamic_index_in_dim(summed, my_grp, 1, keepdims=True)
    arrived = lax.all_to_all(own_share, "dom", split_axis=0, concat_axis=0, tiled=True)
    incoming = arrived.reshape(dom_count, row_slots * col_slots, tile_size)
    local_rows = jnp.arange(row_slots, dtype=jnp.int32) * dom_count + my_dom
    local_cols = jnp.arange(col_slots, dtype=jnp.int32) * grp_count + my_grp
    row_ids = jnp.take(dom_blocks, local_rows, axis=1)
    col_ids = jnp.take(dom_blocks, local_cols, axis=1)
    row_total = NBLK // dom_count
    col_total = NBLK // grp_count
    targets = (
        (row_ids // dom_count)[:, :, None] * col_total + (col_ids // grp_count)[:, None, :]
    ).reshape(-1)
    gathered = (
        jnp.zeros((row_total * col_total, tile_size), jnp.float32)
        .at[targets]
        .add(incoming.reshape(-1, tile_size))
    )
    return (
        gathered.reshape(row_total, col_total, BLK, BLK)
        .transpose(0, 2, 1, 3)
        .reshape(row_total * BLK, col_total * BLK)
    )


def solution(mesh):
    return jax.shard_map(
        local,
        mesh=mesh,
        in_specs=(
            P(("dom", "grp"), None, None),
            P(("dom", "grp"), None),
            P(("dom", "grp"), None),
            P("dom", "grp"),
            P(),
            P("dom", None, None),
        ),
        out_specs=P("dom", "grp"),
        check_vma=False,
    )
```

profile of v0, /device:TPU:1, one launch (start us, length us, event | category | flops | bytes accessed | tf_op | source)
XLA Modules:
  0.0 939.1 jit_solution(15319914085264817861)
XLA Ops:
  14.4 606.1 %while.16 = (s32[]{:T(128)}, f32[1024,4096]{1,0:T(8,128)}, s32[112,5]{0,1:T(8,128)S(1)}, bf16[112,320,256]{2,1,0:T(8,128)(2,1)}, s32[]{:T(128)}, /*index=5*/f32[...) while((s32[]{:T(128)}, f32[1024,4096]{1,0:T(8,128)}, s32[112,5]{0,1:T(8,128)S(1)}, ...), condition=%wide.region_2.3_spmd, body=%wide.region_0.2_spmd.sunk | while | flops 422220704 | bytes 35422096 | solution.py:47
  28.5 8.1 copy.34
  41.6 16.1 %scatter_fusion = f32[1024,4096]{1,0:T(8,128)} fusion(f32[1024,4096]{1,0:T(8,128)} %get-tuple-element.280, s32[200]{0:T(256)S(1)} %bitcast.51, f32[200,4096]{1,0:T(8,128)S(1)} %reshape.369), kind=kCustom, calls=%fused_computation.2.clone.1 | custom fusion | flops 819200 | bytes 9831200 | tf_op jit(solution)/shard_map/while/body/eval_jaxpr/scatter-add | solution.py:45
  71.8 8.1 copy.34
  84.9 16.1 %scatter_fusion = f32[1024,4096]{1,0:T(8,128)} fusion(f32[1024,4096]{1,0:T(8,128)} %get-tuple-element.280, s32[200]{0:T(256)S(1)} %bitcast.51, f32[200,4096]{1,0:T(8,128)S(1)} %reshape.369), kind=kCustom, calls=%fused_computation.2.clone.1 | custom fusion | flops 819200 | bytes 9831200 | tf_op jit(solution)/shard_map/while/body/eval_jaxpr/scatter-add | solution.py:45
  115.1 8.1 copy.34
  128.2 16.1 %scatter_fusion = f32[1024,4096]{1,0:T(8,128)} fusion(f32[1024,4096]{1,0:T(8,128)} %get-tuple-element.280, s32[200]{0:T(256)S(1)} %bitcast.51, f32[200,4096]{1,0:T(8,128)S(1)} %reshape.369), kind=kCustom, calls=%fused_computation.2.clone.1 | custom fusion | flops 819200 | bytes 9831200 | tf_op jit(solution)/shard_map/while/body/eval_jaxpr/scatter-add | solution.py:45
  158.4 8.1 copy.34
  171.5 16.1 %scatter_fusion = f32[1024,4096]{1,0:T(8,128)} fusion(f32[1024,4096]{1,0:T(8,128)} %get-tuple-element.280, s32[200]{0:T(256)S(1)} %bitcast.51, f32[200,4096]{1,0:T(8,128)S(1)} %reshape.369), kind=kCustom, calls=%fused_computation.2.clone.1 | custom fusion | flops 819200 | bytes 9831200 | tf_op jit(solution)/shard_map/while/body/eval_jaxpr/scatter-add | solution.py:45
  201.6 8.1 copy.34
  214.7 16.1 %scatter_fusion = f32[1024,4096]{1,0:T(8,128)} fusion(f32[1024,4096]{1,0:T(8,128)} %get-tuple-element.280, s32[200]{0:T(256)S(1)} %bitcast.51, f32[200,4096]{1,0:T(8,128)S(1)} %reshape.369), kind=kCustom, calls=%fused_computation.2.clone.1 | custom fusion | flops 819200 | bytes 9831200 | tf_op jit(solution)/shard_map/while/body/eval_jaxpr/scatter-add | solution.py:45
  244.9 8.1 copy.34
  258.0 16.1 %scatter_fusion = f32[1024,4096]{1,0:T(8,128)} fusion(f32[1024,4096]{1,0:T(8,128)} %get-tuple-element.280, s32[200]{0:T(256)S(1)} %bitcast.51, f32[200,4096]{1,0:T(8,128)S(1)} %reshape.369), kind=kCustom, calls=%fused_computation.2.clone.1 | custom fusion | flops 819200 | bytes 9831200 | tf_op jit(solution)/shard_map/while/body/eval_jaxpr/scatter-add | solution.py:45
  288.1 8.1 copy.34
  301.2 16.1 %scatter_fusion = f32[1024,4096]{1,0:T(8,128)} fusion(f32[1024,4096]{1,0:T(8,128)} %get-tuple-element.280, s32[200]{0:T(256)S(1)} %bitcast.51, f32[200,4096]{1,0:T(8,128)S(1)} %reshape.369), kind=kCustom, calls=%fused_computation.2.clone.1 | custom fusion | flops 819200 | bytes 9831200 | tf_op jit(solution)/shard_map/while/body/eval_jaxpr/scatter-add | solution.py:45
  331.4 8.1 copy.34
  344.5 16.1 %scatter_fusion = f32[1024,4096]{1,0:T(8,128)} fusion(f32[1024,4096]{1,0:T(8,128)} %get-tuple-element.280, s32[200]{0:T(256)S(1)} %bitcast.51, f32[200,4096]{1,0:T(8,128)S(1)} %reshape.369), kind=kCustom, calls=%fused_computation.2.clone.1 | custom fusion | flops 819200 | bytes 9831200 | tf_op jit(solution)/shard_map/while/body/eval_jaxpr/scatter-add | solution.py:45
  387.8 16.1 %scatter_fusion = f32[1024,4096]{1,0:T(8,128)} fusion(f32[1024,4096]{1,0:T(8,128)} %get-tuple-element.280, s32[200]{0:T(256)S(1)} %bitcast.51, f32[200,4096]{1,0:T(8,128)S(1)} %reshape.369), kind=kCustom, calls=%fused_computation.2.clone.1 | custom fusion | flops 819200 | bytes 9831200 | tf_op jit(solution)/shard_map/while/body/eval_jaxpr/scatter-add | solution.py:45
  418.1 8.1 copy.34
  431.1 16.1 %scatter_fusion = f32[1024,4096]{1,0:T(8,128)} fusion(f32[1024,4096]{1,0:T(8,128)} %get-tuple-element.280, s32[200]{0:T(256)S(1)} %bitcast.51, f32[200,4096]{1,0:T(8,128)S(1)} %reshape.369), kind=kCustom, calls=%fused_computation.2.clone.1 | custom fusion | flops 819200 | bytes 9831200 | tf_op jit(solution)/shard_map/while/body/eval_jaxpr/scatter-add | solution.py:45
  474.4 16.1 %scatter_fusion = f32[1024,4096]{1,0:T(8,128)} fusion(f32[1024,4096]{1,0:T(8,128)} %get-tuple-element.280, s32[200]{0:T(256)S(1)} %bitcast.51, f32[200,4096]{1,0:T(8,128)S(1)} %reshape.369), kind=kCustom, calls=%fused_computation.2.clone.1 | custom fusion | flops 819200 | bytes 9831200 | tf_op jit(solution)/shard_map/while/body/eval_jaxpr/scatter-add | solution.py:45
  517.6 16.1 %scatter_fusion = f32[1024,4096]{1,0:T(8,128)} fusion(f32[1024,4096]{1,0:T(8,128)} %get-tuple-element.280, s32[200]{0:T(256)S(1)} %bitcast.51, f32[200,4096]{1,0:T(8,128)S(1)} %reshape.369), kind=kCustom, calls=%fused_computation.2.clone.1 | custom fusion | flops 819200 | bytes 9831200 | tf_op jit(solution)/shard_map/while/body/eval_jaxpr/scatter-add | solution.py:45
  547.9 8.1 copy.34
  560.9 16.1 %scatter_fusion = f32[1024,4096]{1,0:T(8,128)} fusion(f32[1024,4096]{1,0:T(8,128)} %get-tuple-element.280, s32[200]{0:T(256)S(1)} %bitcast.51, f32[200,4096]{1,0:T(8,128)S(1)} %reshape.369), kind=kCustom, calls=%fused_computation.2.clone.1 | custom fusion | flops 819200 | bytes 9831200 | tf_op jit(solution)/shard_map/while/body/eval_jaxpr/scatter-add | solution.py:45
  591.3 8.1 copy.34
  604.4 16.1 %scatter_fusion = f32[1024,4096]{1,0:T(8,128)} fusion(f32[1024,4096]{1,0:T(8,128)} %get-tuple-element.280, s32[200]{0:T(256)S(1)} %bitcast.51, f32[200,4096]{1,0:T(8,128)S(1)} %reshape.369), kind=kCustom, calls=%fused_computation.2.clone.1 | custom fusion | flops 819200 | bytes 9831200 | tf_op jit(solution)/shard_map/while/body/eval_jaxpr/scatter-add | solution.py:45
  621.1 11.7 %broadcast_multiply_fusion = f32[1024,4096]{1,0:T(8,128)} fusion(f32[1024,4096]{1,0:T(8,128)} %get-tuple-element.195, f32[1024]{0:T(1024)S(1)} %convert_element_type.42), kind=kLoop, calls=%fused_computation.27 | loop fusion | flops 4194304 | bytes 33558528 | tf_op jit(solution)/shard_map/mul | solution.py:56
  634.3 222.3 %all-reduce.2.cloned.1.call-done = f32[8,16,8,4096]{3,2,1,0:T(8,128)} async-done(((f32[8,16,8,4096]{3,2,1,0:T(8,128)}), f32[8,16,8,4096]{3,2,1,0:T(8,128)}) %all-reduce.2.cloned.1.call-update) | async-done | bytes 16777232 | tf_op jit(solution)/shard_map/psum | solution.py:58
  865.3 14.1 %all-to-all-done = f32[8,1,8,4096]{3,2,1,0:T(8,128)S(1)} async-done(((f32[8,1,8,4096]{3,2,1,0:T(8,128)}), f32[8,1,8,4096]{3,2,1,0:T(8,128)S(1)}, u32[]{:S(2)}, u32[]{:S(2)}) %all-to-all-start) | async-done | bytes 1048608 | tf_op jit(solution)/shard_map/all_to_all | solution.py:60
  885.2 14.2 %reshape.323 = f32[32,16,64,64]{3,2,1,0:T(8,128)} reshape(f32[512,4096]{1,0:T(8,128)} %scatter_custom_fusion.1) | data formatting | bytes 16777216 | tf_op jit(solution)/shard_map/reshape | solution.py:77
  899.4 18.4 %copy.29 = f32[32,64,16,64]{3,2,1,0:T(8,128)} copy(f32[32,64,16,64]{3,1,2,0:T(8,128)} %bitcast.49) | data formatting | bytes 16777216 | tf_op jit(solution)/shard_map/transpose | solution.py:78
  917.8 14.5 %reshape.324 = f32[2048,1024]{1,0:T(8,128)} reshape(f32[32,64,16,64]{3,2,1,0:T(8,128)} %copy.29) | data formatting | bytes 16777216 | tf_op jit(solution)/shard_map/reshape | solution.py:79
  (189 shorter events, 314.7 us)
Async XLA Ops:
  6.5 850.1 %all-reduce.2.cloned.1.call-start = ((), (), s32[]{:S(2)}) async-start(), calls=%async_computation.1 | async-start | bytes 33554432 | tf_op jit(solution)/shard_map/psum | solution.py:58
  6.5 7.8 copy-start
  14.4 606.1 %copy-start.1 = (s32[1,32,32]{2,1,0:T(8,128)S(1)}, s32[1,32,32]{2,1,0:T(8,128)}, u32[]{:S(2)}) copy-start(s32[1,32,32]{2,1,0:T(8,128)} %param.13) | copy-start | bytes 12292
  632.9 0.7 copy-start.2
  858.9 20.5 %all-to-all-start = ((f32[8,1,8,4096]{3,2,1,0:T(8,128)}), f32[8,1,8,4096]{3,2,1,0:T(8,128)S(1)}, u32[]{:S(2)}, u32[]{:S(2)}) async-start(f32[8,1,8,4096]{3,2,1,0:T(8,128)} %constant_dynamic-slice_fusion.1), calls=%async_computation | async-start | bytes 2097152 | tf_op jit(solution)/shard_map/all_to_all | solution.py:60
Sparse Core Ops, SparseCore 0:
  633.0 223.5 all-reduce.1
where the time goes:
time: 945 us; the launch traced here: 939 us
  local copies, waits for them, and re-layouts  354 us (37%)
  other arithmetic  265 us (28%)
  waiting for transfers between devices  236 us (25%)
  matrix products  63.7 us (7%)
  between operations  13.4 us (1%)
    scatter-add x14, other arithmetic, accumulate(): return partial_value.at[targets].add(tiles)  226 us
    psum x1, waiting for transfers between devices, local(): summed = lax.psum(partial_value, 'grp')  222 us
    transpose x14, local copies, waits for them, and re-layouts, accumulate(): tiles = product.reshape(group_size, NBT, BLK, NBT, BLK).transpose(0, 1, 3...  114 us
    reshape x14, local copies, waits for them, and re-layouts, accumulate(): product.reshape(group_size, NBT, BLK, NBT, BLK).transpose(0, 1, 3, 2, 4)  108 us
    reshape x14, local copies, waits for them, and re-layouts, accumulate(): tiles = product.reshape(group_size, NBT, BLK, NBT, BLK).transpose(0, 1, 3...  69.3 us
    dot_general x14, matrix products, accumulate(): jnp.einsum('bfp,bgp->bfg', values, scaled, preferred_element_type=jnp.flo...  63.7 us
  transfers between devices with their start and end apart: 2, of which 2 were waited for; matrix products, arithmetic and copies ran while one was open for 0% of the time, Pallas kernels for 0%

commit v1 on v0

v1 whole, which is shorter than its diff:
```python
import numpy as np
import jax
import jax.numpy as jnp
from jax import lax
from jax.experimental import pallas as pl
from jax.experimental.pallas import tpu as pltpu
from jax.sharding import PartitionSpec as P

SLOTS = 112
TILES = 272
UNROLL = 8
CHUNK = 8


def place_table():
    table = np.zeros((32, 16), np.int32)
    for key in range(32):
        a, h = key // 2, key % 2
        for b in range(16):
            d = abs(b - a)
            lo, hi = min(a, b), max(a, b)
            if d == 8:
                table[key, b] = 256 + (lo if h == 0 else hi)
            else:
                owner, delta = (hi, d) if d < 8 else (lo, 16 - d)
                table[key, b] = delta // 2 * 64 + owner * 4 + delta % 2 * 2 + h
    return table.reshape(-1)


def sort5(v):
    v = list(v)
    for i, j in ((0, 1), (3, 4), (2, 4), (2, 3), (1, 4), (0, 3), (0, 2), (1, 3), (1, 2)):
        low, high = jnp.minimum(v[i], v[j]), jnp.maximum(v[i], v[j])
        v[i], v[j] = low, high
    return v


def products_kernel(table, blocks, live, weights, basis, out, vbuf, acc, spad, sems, out_sem):
    count = live[0, 0]

    def load(c):
        return pltpu.make_async_copy(
            basis.at[pl.ds(c * CHUNK, CHUNK)], vbuf.at[pl.ds(c * CHUNK, CHUNK)], sems.at[c]
        )

    @pl.loop(0, SLOTS // CHUNK)
    def _(c):
        @pl.when(c * CHUNK < count)
        def _():
            load(c).start()

    @pl.loop(0, TILES, step=4)
    def _(n):
        for k in range(4):
            acc[n + k] = jnp.zeros((64, 128), jnp.float32)

    def batch(b, u):
        packed = []
        for i in range(5):
            p = blocks[b, i]
            packed.append((((p & 15) << 1) + (p >> 4)) * 8 + i)
        packed = sort5(packed)
        key = [v >> 3 for v in packed]
        half = [v & 1 for v in key]
        cls = [v >> 1 for v in key]
        row = [v << 4 for v in key]
        w = weights[pl.ds(b, 1), :] * jnp.where(b < count, 1.0, 0.0)
        values = []
        for i in range(5):
            v = vbuf[b, pl.ds(pl.multiple_of((packed[i] & 7) * 64, 64), 64), :]
            values.append(v)
            s = (v.astype(jnp.float32) * w).astype(jnp.bfloat16)
            spad[u, pl.ds(pl.multiple_of(i * 128 + half[i] * 64, 64), 64), :] = s
            spad[u, pl.ds(pl.multiple_of(i * 128 + 64 - half[i] * 64, 64), 64), :] = jnp.zeros_like(s)
        for first, cols in ((0, 2), (2, 2), (4, 1)):
            rows = first + cols
            lhs = jnp.concatenate(values[:rows], axis=0)
            rhs = spad[u, first * 128 : (first + cols) * 128, :]
            prod = lax.dot_general(lhs, rhs, (((1,), (1,)), ((), ())), preferred_element_type=jnp.float32)
            for c in range(cols):
                j = first + c
                spots, sums = [], []
                for i in range(j + 1):
                    spot = table[row[i] + cls[j]]
                    spots.append(spot)
                    sums.append(acc[spot] + prod[i * 64 : i * 64 + 64, c * 128 : c * 128 + 128])
                for spot, value in zip(spots, sums):
                    acc[spot] = value

    @pl.loop(0, pl.cdiv(count, UNROLL))
    def _(n):
        @pl.when(lax.rem(n * UNROLL, CHUNK) == 0)
        def _():
            load(n * UNROLL // CHUNK).wait()

        for u in range(UNROLL):
            batch(n * UNROLL + u, u)

    done = pltpu.make_async_copy(acc, out, out_sem)
    done.start()
    done.wait()


def products(basis_values, point_weights, batch_blocks, live_count):
    smem = pl.BlockSpec(memory_space=pltpu.SMEM)
    return pl.pallas_call(
        products_kernel,
        out_shape=jax.ShapeDtypeStruct((TILES, 64, 128), jnp.float32),
        in_specs=[smem, smem, smem, pl.BlockSpec(memory_space=pltpu.VMEM), pl.BlockSpec(memory_space=pl.ANY)],
        out_specs=pl.BlockSpec(memory_space=pl.ANY),
        scratch_shapes=[
            pltpu.VMEM((SLOTS, 320, 256), jnp.bfloat16),
            pltpu.VMEM((TILES, 64, 128), jnp.float32),
            pltpu.VMEM((UNROLL, 640, 256), jnp.bfloat16),
            pltpu.SemaphoreType.DMA((SLOTS // CHUNK,)),
            pltpu.SemaphoreType.DMA,
        ],
        compiler_params=pltpu.CompilerParams(vmem_limit_bytes=60 * 2**20),
        name="products",
    )(jnp.asarray(place_table()), batch_blocks, live_count, point_weights, basis_values)


MESH = pl.DeviceIdType.MESH
X_FIRST = (True, False, True, False, True, False)


def exchange_kernel(mask, partial, out, relay, direct, final, stage, relay2, direct2, final2, half_sum,
                    send, send_half, sem1, sem2, send1, send2, arrive, leave):
    dom, grp = lax.axis_index("dom"), lax.axis_index("grp")
    x, z = grp % 4, grp // 4

    def at(first, second, x_first):
        return second * 4 + first if x_first else first * 4 + second

    barrier = pltpu.get_barrier_semaphore()
    peers = [(dom, z * 4 + (x + 1) % 4), (dom, z * 4 + (x + 3) % 4),
             (dom, (z + 1) % 4 * 4 + x), (dom, (z + 3) % 4 * 4 + x)]
    peers += [((dom + n) % 8, grp) for n in range(1, 8)]
    source = (grp + 1 + (dom - grp - 1) % 8) % 16
    peers += [(n, source) for n in range(8)]
    for peer in peers:
        pl.semaphore_signal(barrier, inc=1, device_id=peer, device_id_type=MESH)
    pl.semaphore_wait(barrier, len(peers))

    def piece(k, owner, h):
        if k < 4:
            return partial.at[pl.ds(64 * k + 4 * owner + 2 * h, 2)]
        return partial.at[pl.ds(256 + owner, 1), pl.ds((k - 4) * 32 + 16 * h, 16), :]

    def view(buffers, k, *index):
        return buffers[k // 4].at[(k % 4, *index)]

    def remote(src, dst, send_sem, recv_sem, peer):
        return pltpu.make_async_remote_copy(src_ref=src, dst_ref=dst, send_sem=send_sem, recv_sem=recv_sem,
                                            device_id=peer, device_id_type=MESH)

    def copies1(k, s):
        xf = X_FIRST[k]
        mf = x if xf else z
        right, left, far = (mf + 1) % 4, (mf + 3) % 4, (mf + 2) % 4
        ms = z if xf else x
        so = (ms + s) % 4
        to_right = (dom, at(right, ms, xf))
        to_left = (dom, at(left, ms, xf))

        specs = [
            (piece(k, at(far, so, xf), 0), view(relay, k, s, 0), to_right),
            (piece(k, at(far, so, xf), 1), view(relay, k, s, 1), to_left),
            (piece(k, at(right, so, xf), 1), view(direct, k, s, 1), to_right),
            (piece(k, at(left, so, xf), 0), view(direct, k, s, 0), to_left),
            (view(relay, k, s, 0), view(final, k, s, 0), to_right),
            (view(relay, k, s, 1), view(final, k, s, 1), to_left),
        ]

        def copy(n):
            src, dst, peer = specs[n]
            return remote(src, dst, send1.at[k, s, n], sem1.at[k, s, n], peer)

        return copy, (right, left, mf, so, xf)

    def copies2(k):
        xf = X_FIRST[k]
        mf, ms = (x, z) if xf else (z, x)
        to_right = (dom, at(mf, (ms + 1) % 4, xf))
        to_left = (dom, at(mf, (ms + 3) % 4, xf))

        specs = [
            (view(stage, k, 2, 0), view(relay2, k, 0), to_right),
            (view(stage, k, 2, 1), view(relay2, k, 1), to_left),
            (view(stage, k, 1, 1), view(direct2, k, 1), to_right),
            (view(stage, k, 3, 0), view(direct2, k, 0), to_left),
            (view(relay2, k, 0), view(final2, k, 0), to_right),
            (view(relay2, k, 1), view(final2, k, 1), to_left),
        ]

        def copy(n):
            src, dst, peer = specs[n]
            return remote(src, dst, send2.at[k, n], sem2.at[k, n], peer)

        return copy

    ORDER = (2, 1, 3, 0)

    def begin(ks):
        for s in ORDER:
            for k in ks:
                c, _ = copies1(k, s)
                c(0).start()
                c(1).start()
        for s in ORDER:
            for k in ks:
                c, _ = copies1(k, s)
                c(2).start()
                c(3).start()

    def pass_on(ks):
        for s in ORDER:
            for k in ks:
                c, (right, left, mf, so, xf) = copies1(k, s)
                for h, owner in ((0, right), (1, left)):
                    c(h).wait_recv()
                    slot = view(relay, k, s, h)
                    slot[...] = slot[...] + piece(k, at(owner, so, xf), h)[...]
                    c(4 + h).start()

    def settle(ks):
        for s in ORDER:
            for k in ks:
                c, (right, left, mf, so, xf) = copies1(k, s)
                for h in (0, 1):
                    c(4 + h).wait_recv()
                    c(3 - h).wait_recv()
                    view(stage, k, s, h)[...] = (
                        piece(k, at(mf, so, xf), h)[...] + view(final, k, s, h)[...] + view(direct, k, s, h)[...]
                    )
            for k in ks:
                c = copies2(k)
                if s == 2:
                    c(0).start()
                    c(1).start()
                if s == 1:
                    c(2).start()
                if s == 3:
                    c(3).start()

    def pass_on2(ks):
        for k in ks:
            c = copies2(k)
            for h, s in ((0, 1), (1, 3)):
                c(h).wait_recv()
                slot = view(relay2, k, h)
                slot[...] = slot[...] + view(stage, k, s, h)[...]
                c(4 + h).start()

    def settle2(ks):
        for k in ks:
            c = copies2(k)
            for h in (0, 1):
                c(4 + h).wait_recv()
                c(3 - h).wait_recv()
                value = view(stage, k, 0, h)[...] + view(final2, k, h)[...] + view(direct2, k, h)[...]
                if k < 4:
                    hand_out(2 * k + h, value.reshape(128, 128))
                else:
                    half_sum[(k - 4) * 32 + 16 * h : (k - 4) * 32 + 16 * h + 16, :] = value[0]

    lane = lax.broadcasted_iota(jnp.int32, (64, 128), 1)
    low_half = lax.broadcasted_iota(jnp.int32, (128, 128), 1) < 64
    top_half = lax.broadcasted_iota(jnp.int32, (128, 128), 0) < 64

    def factor(p, q):
        return mask[0, p, q].astype(jnp.float32)

    def kept(row, col):
        halves = [jnp.where(lane < 64, factor(row + 16 * i, col), factor(row + 16 * i, col + 16)) for i in (0, 1)]
        return jnp.concatenate(halves, axis=0)

    def to_group(src, a, rows, n):
        target = a % 8
        dst = out.at[dom, a // 8, rows]

        @pl.when(target != dom)
        def _():
            remote(src, dst, leave.at[0, n], arrive.at[dom, a // 8], (target, grp)).start()

        @pl.when(target == dom)
        def _():
            pltpu.make_async_copy(src, dst, arrive.at[dom, a // 8]).start()

    def to_other(src, a, rows, n):
        dst = out.at[dom, grp // 8, rows]
        return remote(src, dst, leave.at[1, n], arrive.at[dom, grp // 8], (grp % 8, a))

    whole = pl.ds(0, 128)

    def hand_out(n, value):
        a = (grp + 16 - n) % 16
        turned = value.T
        if n == 0:
            send[0, 0] = jnp.where(top_half | ~low_half, value, turned) * kept(a, grp)
            to_group(send.at[0, 0], a, whole, 0)
            return
        wrapped = grp < n
        send[0, n] = jnp.where(wrapped, turned, value) * kept(a, grp)
        to_group(send.at[0, n], a, whole, n)
        send[1, n] = jnp.where(wrapped, value, turned) * kept(grp, a)
        to_other(send.at[1, n], a, whole, n).start()

    def hand_out_half():
        a = (grp + 8) % 16
        h = grp // 8
        low, high = grp % 8, grp % 8 + 8
        value = half_sum[...]
        upper = value * jnp.where(lane < 64, factor(low + 16 * h, high), factor(low + 16 * h, high + 16))
        lower = value * jnp.where(lane < 64, factor(high, low + 16 * h), factor(high + 16, low + 16 * h))
        rows = pl.ds(pl.multiple_of(h * 64, 64), 64)
        send_half[0] = jnp.where(h == 0, lower, upper)
        to_group(send_half.at[0], a, rows, 8)
        send_half[1] = jnp.where(h == 0, upper, lower)
        to_other(send_half.at[1], a, rows, 8).start()

    first, last = (0, 1), (4, 5, 2, 3)
    begin(first)
    pass_on(first)
    begin(last)
    settle(first)
    pass_on(last)
    pass_on2(first)
    settle2(first)
    settle(last)
    pass_on2(last)
    settle2(last)
    hand_out_half()

    for k in range(6):
        for s in range(4):
            for n in range(6):
                copies1(k, s)[0](n).wait_send()
        for n in range(6):
            copies2(k)(n).wait_send()
    for n in range(9):
        a = (grp + 16 - n) % 16
        src = send_half if n == 8 else send.at[:, n]
        rows = pl.ds(0, 64) if n == 8 else whole

        @pl.when(a % 8 != dom)
        def _():
            remote(src.at[0], out.at[dom, a // 8, rows], leave.at[0, n], arrive.at[dom, a // 8], (a % 8, grp)).wait_send()

        if n:
            to_other(src.at[1], a, rows, n).wait_send()
    for d in range(8):
        for t in range(2):
            pltpu.make_async_copy(out.at[d, t], out.at[d, t], arrive.at[d, t]).wait()


def exchange(partial, pair_mask):
    def pair(*lead):
        return [pltpu.VMEM((4, *lead, 2, 64, 128), jnp.float32), pltpu.VMEM((2, *lead, 1, 16, 128), jnp.float32)]

    buffers = [pair(4, 2), pair(4, 2), pair(4, 2), pair(4, 2), pair(2), pair(2), pair(2)]
    flat = [b for two in buffers for b in two]
    rest = [
        pltpu.VMEM((64, 128), jnp.float32),
        pltpu.VMEM((2, 8, 128, 128), jnp.float32),
        pltpu.VMEM((2, 64, 128), jnp.float32),
        pltpu.SemaphoreType.DMA((6, 4, 6)),
        pltpu.SemaphoreType.DMA((6, 6)),
        pltpu.SemaphoreType.DMA((6, 4, 6)),
        pltpu.SemaphoreType.DMA((6, 6)),
        pltpu.SemaphoreType.DMA((8, 2)),
        pltpu.SemaphoreType.DMA((2, 9)),
    ]

    def body(mask, partial, out, *refs):
        pairs = [refs[2 * n : 2 * n + 2] for n in range(7)]
        exchange_kernel(mask, partial, out, *pairs, *refs[14:])

    return pl.pallas_call(
        body,
        out_shape=jax.ShapeDtypeStruct((8, 2, 128, 128), jnp.float32),
        in_specs=[pl.BlockSpec(memory_space=pltpu.SMEM), pl.BlockSpec(memory_space=pltpu.VMEM)],
        out_specs=pl.BlockSpec(memory_space=pl.ANY),
        scratch_shapes=flat + rest,
        compiler_params=pltpu.CompilerParams(
            collective_id=0, has_side_effects=True, vmem_limit_bytes=48 * 2**20
        ),
        name="exchange",
    )(pair_mask, partial)


def place_kernel(ids, tiles, out, image, sem):
    dom, grp = lax.axis_index("dom"), lax.axis_index("grp")

    @pl.loop(0, 2048, step=64)
    def _(n):
        image[pl.ds(pl.multiple_of(n, 64), 64), :] = jnp.zeros((64, 1024), jnp.float32)

    left = lax.broadcasted_iota(jnp.int32, (64, 128), 1) < 64

    @pl.loop(0, 8)
    def _(d):
        for t in range(2):
            quad = tiles[d, t]
            if t == 1:
                turn = jnp.logical_and(grp < 8, dom == grp)
                quad = jnp.where(turn, quad.T, quad)
            for i in range(2):
                row = ids[d, dom + 8 * t + 16 * i] // 8
                part = quad[64 * i : 64 * i + 64]
                other = jnp.concatenate([part[:, 64:], part[:, :64]], axis=1)
                for j in range(2):
                    col = ids[d, grp + 16 * j] // 16
                    half = col % 2
                    value = jnp.where(half == j, part, other)
                    value = jnp.where(left == (half == 0), value, 0.0)
                    spot = (pl.ds(pl.multiple_of(row * 64, 64), 64), pl.ds(pl.multiple_of(col // 2 * 128, 128), 128))
                    image[spot] = image[spot] + value

    done = pltpu.make_async_copy(image, out, sem)
    done.start()
    done.wait()


def place(dom_blocks, tiles):
    return pl.pallas_call(
        place_kernel,
        out_shape=jax.ShapeDtypeStruct((2048, 1024), jnp.float32),
        in_specs=[pl.BlockSpec(memory_space=pltpu.SMEM), pl.BlockSpec(memory_space=pltpu.VMEM)],
        out_specs=pl.BlockSpec(memory_space=pl.ANY),
        scratch_shapes=[pltpu.VMEM((2048, 1024), jnp.float32), pltpu.SemaphoreType.DMA],
        compiler_params=pltpu.CompilerParams(vmem_limit_bytes=24 * 2**20),
        name="place",
    )(dom_blocks, tiles)


def local(basis_values, point_weights, batch_blocks, live_count, dom_blocks, pair_mask):
    partial = products(basis_values, point_weights, batch_blocks, live_count)
    tiles = exchange(partial, pair_mask)
    return place(dom_blocks, tiles)


def solution(mesh):
    return jax.shard_map(
        local,
        mesh=mesh,
        in_specs=(
            P(("dom", "grp"), None, None),
            P(("dom", "grp"), None),
            P(("dom", "grp"), None),
            P("dom", "grp"),
            P(),
            P("dom", None, None),
        ),
        out_specs=P("dom", "grp"),
        check_vma=False,
    )
```

time: 945 us -> 128 us (0.14)
  local copies, waits for them, and re-layouts: 354 us -> 1.42 us
  other arithmetic: 265 us -> 0 us
  waiting for transfers between devices: 236 us -> 0 us
  Pallas kernels: 0 us -> 123 us
  matrix products: 63.7 us -> 0 us
  between operations: 13.4 us -> 0.69 us
    scatter-add x15 -> x0, other arithmetic: 232 us -> none  [the longest x14 226 us: accumulate(): return partial_value.at[targets].add(tiles)]
    psum x1 -> x0, waiting for transfers between devices: 222 us -> none  [local(): summed = lax.psum(partial_value, 'grp')]
    reshape x30 -> x0, local copies, waits for them, and re-layouts: 206 us -> none  [the longest x14 108 us: accumulate(): product.reshape(group_size, NBT, BLK, NBT, BLK).transpose(0, 1, 3, 2, 4)]
    transpose x15 -> x0, local copies, waits for them, and re-layouts: 132 us -> none  [the longest x14 114 us: accumulate(): tiles = product.reshape(group_size, NBT, BLK, NBT, BLK).transpose(0, 1, 3...]
    pallas_call x0 -> x3, Pallas kernels: none -> 123 us  [the longest x1 100 us: exchange(): pl.pallas_call(body, out_shape=jax.ShapeDtypeStruct((8, 2, 128, 128), jnp...]
    dot_general x14 -> x0, matrix products: 63.7 us -> none  [accumulate(): jnp.einsum('bfp,bgp->bfg', values, scaled, preferred_element_type=jnp.flo...]
    all_to_all x1 -> x0, waiting for transfers between devices: 14.1 us -> none  [local(): lax.all_to_all(own_share, 'dom', split_axis=0, concat_axis=0, tiled=True)]
    mul x16 -> x0, other arithmetic: 12 us -> none  [the longest x1 11.7 us: local(): partial_value = partial_value * mask_local[:, None].astype(jnp.float32)]
  transfers between devices with their start and end apart: 2 -> 0, of which waited for: 2 -> 0; matrix products, arithmetic and copies ran while one was open for 0% -> 0% of each run, Pallas kernels for 0% -> 0%
where the time goes in v1:
time: 128 us; the launch traced here: 126 us
  Pallas kernels  123 us (96%)
  local copies, waits for them, and re-layouts  1.42 us (1%)
    pallas_call x1, Pallas kernels, exchange(): pl.pallas_call(body, out_shape=jax.ShapeDtypeStruct((8, 2, 128, 128), jnp...  100 us
    pallas_call x1, Pallas kernels, products(): pl.pallas_call(products_kernel, out_shape=jax.ShapeDtypeStruct((TILES, 64...  17 us
    pallas_call x1, Pallas kernels, place(): pl.pallas_call(place_kernel, out_shape=jax.ShapeDtypeStruct((2048, 1024),...  6.06 us

profile of v1, /device:TPU:1, one launch (start us, length us, event | category | flops | bytes accessed | tf_op | source)
XLA Modules:
  0.0 125.6 jit_solution(17060121040946582732)
XLA Ops:
  0.7 1.4 %copy.8.blocks = s32[112,5]{1,0:T(8,128)} copy(s32[112,5]{0,1:T(8,128)} %param.9) | data formatting | bytes 4480 | tf_op args[2]
  2.1 0.0 copy-start
  2.1 17.0 %products.1.partial = f32[272,64,128]{2,1,0:T(8,128)} custom-call(s32[512]{0:T(512)} %constant.2.clone.table, s32[112,5]{1,0:T(8,128)} %copy.8.blocks, s32[1,1]{1,0:T(1,128)S(6)} %copy.9.live, f32[112,256]{1,0:T(8,128)} %weights.1, bf16[112,320,256]{2,1,0:T(8,128)(2,1)} %basis.1), custom_call_target="tpu_custom_call" | custom-call | tf_op jit(solution)/shard_map/products/pallas_call | solution.py:106
  19.1 0.0 copy-done
  19.1 0.0 copy-start.1
  19.1 100.4 %exchange.1.tiles = f32[8,2,128,128]{3,2,1,0:T(8,128)S(1)} custom-call(s32[1,32,32]{2,1,0:T(8,128)S(1)} %copy-done, f32[272,64,128]{2,1,0:T(8,128)} %products.1.partial), custom_call_target="tpu_custom_call" | custom-call | tf_op jit(solution)/shard_map/exchange/pallas_call | solution.py:379
  119.5 0.0 copy-done.1
  119.5 6.1 %place.1 = f32[2048,1024]{1,0:T(8,128)} custom-call(s32[8,32]{1,0:T(8,128)S(1)} %copy-done.1, f32[8,2,128,128]{3,2,1,0:T(8,128)S(1)} %exchange.1.tiles), custom_call_target="tpu_custom_call" | custom-call | tf_op jit(solution)/shard_map/place/pallas_call | solution.py:426
Async XLA Ops:
  2.1 17.0 %copy-start = (s32[1,32,32]{2,1,0:T(8,128)S(1)}, s32[1,32,32]{2,1,0:T(8,128)}, u32[]{:S(2)}) copy-start(s32[1,32,32]{2,1,0:T(8,128)} %mask.1) | copy-start | bytes 12292
  19.1 100.4 %copy-start.1 = (s32[8,32]{1,0:T(8,128)S(1)}, s32[8,32]{1,0:T(8,128)}, u32[]{:S(2)}) copy-start(s32[8,32]{1,0:T(8,128)} %ids.1) | copy-start | bytes 3076

commit v2 on v1

--- a/solution.py
+++ b/solution.py
@@ -12,6 +12,13 @@
 CHUNK = 8
 
 
+SLABS = ((True, (1, 8), (2,)), (False, (3,), (4,)), (True, (5,), (6,)), (False, (7,), (0,)))
+SIZES = tuple(tuple(sum(1 if q == 8 else 2 for q in half) for half in slab[1:]) for slab in SLABS)
+ROUNDS = ((0, 1), (2, 3))
+BASES = tuple(16 * sum(sum(n) for n in SIZES[:k]) for k in range(len(SLABS)))
+X_FIRST = tuple(slab[0] for slab in SLABS)
+
+
 def place_table():
     table = np.zeros((32, 16), np.int32)
     for key in range(32):
@@ -19,11 +26,14 @@
         for b in range(16):
             d = abs(b - a)
             lo, hi = min(a, b), max(a, b)
+            owner, delta = (hi, d) if d < 8 else (lo, 16 - d)
             if d == 8:
-                table[key, b] = 256 + (lo if h == 0 else hi)
-            else:
-                owner, delta = (hi, d) if d < 8 else (lo, 16 - d)
-                table[key, b] = delta // 2 * 64 + owner * 4 + delta % 2 * 2 + h
+                owner = hi if h else lo
+            for k, slab in enumerate(SLABS):
+                quads = slab[1] + slab[2]
+                if delta in quads:
+                    ahead = sum(1 if q == 8 else 2 for q in quads[: quads.index(delta)])
+                    table[key, b] = BASES[k] + owner * sum(SIZES[k]) + ahead + (0 if d == 8 else h)
     return table.reshape(-1)
 
 
@@ -35,7 +45,7 @@
     return v
 
 
-def products_kernel(table, blocks, live, weights, basis, out, vbuf, acc, spad, sems, out_sem):
+def products_kernel(table, blocks, live, weights, basis, out, vbuf, acc, scaled, corner, sems):
     count = live[0, 0]
 
     def load(c):
@@ -49,43 +59,55 @@
         def _():
             load(c).start()
 
-    @pl.loop(0, TILES, step=4)
+    @pl.loop(0, 2 * TILES, step=16)
     def _(n):
-        for k in range(4):
+        for k in range(16):
             acc[n + k] = jnp.zeros((64, 128), jnp.float32)
 
-    def batch(b, u):
+    left = lax.broadcasted_iota(jnp.int32, (64, 128), 1) < 64
+
+    def dot(lhs, rhs):
+        return lax.dot_general(lhs, rhs, (((1,), (1,)), ((), ())), preferred_element_type=jnp.float32)
+
+    def add(spots, parts):
+        sums = [acc[spot] + part for spot, part in zip(spots, parts)]
+        for spot, value in zip(spots, sums):
+            acc[spot] = value
+
+    def half_of(prod, row, col):
+        part = prod[row * 64 : row * 64 + 64, col // 2 * 128 : col // 2 * 128 + 128]
+        return jnp.where(left == (col % 2 == 0), part, 0.0)
+
+    def spot_of(key_i, key_j, col):
+        return table[key_i * 16 + (key_j >> 1)] + ((key_j & 1) ^ (col % 2)) * TILES
+
+    def prepare(b, u):
         packed = []
         for i in range(5):
-            p = blocks[b, i]
+            p = blocks[i, b]
             packed.append((((p & 15) << 1) + (p >> 4)) * 8 + i)
         packed = sort5(packed)
-        key = [v >> 3 for v in packed]
-        half = [v & 1 for v in key]
-        cls = [v >> 1 for v in key]
-        row = [v << 4 for v in key]
         w = weights[pl.ds(b, 1), :] * jnp.where(b < count, 1.0, 0.0)
         values = []
         for i in range(5):
             v = vbuf[b, pl.ds(pl.multiple_of((packed[i] & 7) * 64, 64), 64), :]
             values.append(v)
             s = (v.astype(jnp.float32) * w).astype(jnp.bfloat16)
-            spad[u, pl.ds(pl.multiple_of(i * 128 + half[i] * 64, 64), 64), :] = s
-            spad[u, pl.ds(pl.multiple_of(i * 128 + 64 - half[i] * 64, 64), 64), :] = jnp.zeros_like(s)
-        for first, cols in ((0, 2), (2, 2), (4, 1)):
-            rows = first + cols
-            lhs = jnp.concatenate(values[:rows], axis=0)
-            rhs = spad[u, first * 128 : (first + cols) * 128, :]
-            prod = lax.dot_general(lhs, rhs, (((1,), (1,)), ((), ())), preferred_element_type=jnp.float32)
-            for c in range(cols):
-                j = first + c
-                spots, sums = [], []
-                for i in range(j + 1):
-                    spot = table[row[i] + cls[j]]
-                    spots.append(spot)
-                    sums.append(acc[spot] + prod[i * 64 : i * 64 + 64, c * 128 : c * 128 + 128])
-                for spot, value in zip(spots, sums):
-                    acc[spot] = value
+            if i:
+                scaled[u, i * 64 - 64 : i * 64, :] = s
+            else:
+                corner[u // 4, u % 4 * 64 : u % 4 * 64 + 64, :] = s
+        return [v >> 3 for v in packed], values
+
+    def batch(u, key, values):
+        prod = dot(jnp.concatenate(values, axis=0), scaled[u])
+        for j in range(1, 5):
+            add([spot_of(key[i], key[j], j - 1) for i in range(j + 1)], [half_of(prod, i, j - 1) for i in range(j + 1)])
+
+    def corners(g, keys, values):
+        prod = dot(jnp.concatenate(values, axis=0), corner[g])
+        for c in range(4):
+            add([spot_of(keys[c], keys[c], c)], [half_of(prod, c, c)])
 
     @pl.loop(0, pl.cdiv(count, UNROLL))
     def _(n):
@@ -93,12 +115,18 @@
         def _():
             load(n * UNROLL // CHUNK).wait()
 
-        for u in range(UNROLL):
-            batch(n * UNROLL + u, u)
-
-    done = pltpu.make_async_copy(acc, out, out_sem)
-    done.start()
-    done.wait()
+        for g in range(UNROLL // 4):
+            firsts = []
+            for u in range(4 * g, 4 * g + 4):
+                key, values = prepare(n * UNROLL + u, u)
+                firsts.append((key[0], values[0]))
+                batch(u, key, values)
+            corners(g, [f[0] for f in firsts], [f[1] for f in firsts])
+
+    @pl.loop(0, TILES, step=16)
+    def _(n):
+        for k in range(16):
+            out[n + k] = acc[n + k] + pltpu.roll(acc[n + k + TILES], 64, 1)
 
 
 def products(basis_values, point_weights, batch_blocks, live_count):
@@ -107,48 +135,56 @@
         products_kernel,
         out_shape=jax.ShapeDtypeStruct((TILES, 64, 128), jnp.float32),
         in_specs=[smem, smem, smem, pl.BlockSpec(memory_space=pltpu.VMEM), pl.BlockSpec(memory_space=pl.ANY)],
-        out_specs=pl.BlockSpec(memory_space=pl.ANY),
+        out_specs=pl.BlockSpec(memory_space=pltpu.VMEM),
         scratch_shapes=[
             pltpu.VMEM((SLOTS, 320, 256), jnp.bfloat16),
-            pltpu.VMEM((TILES, 64, 128), jnp.float32),
-            pltpu.VMEM((UNROLL, 640, 256), jnp.bfloat16),
+            pltpu.VMEM((2 * TILES, 64, 128), jnp.float32),
+            pltpu.VMEM((UNROLL, 256, 256), jnp.bfloat16),
+            pltpu.VMEM((UNROLL // 4, 256, 256), jnp.bfloat16),
             pltpu.SemaphoreType.DMA((SLOTS // CHUNK,)),
-            pltpu.SemaphoreType.DMA,
         ],
-        compiler_params=pltpu.CompilerParams(vmem_limit_bytes=60 * 2**20),
+        compiler_params=pltpu.CompilerParams(vmem_limit_bytes=40 * 2**20),
         name="products",
-    )(jnp.asarray(place_table()), batch_blocks, live_count, point_weights, basis_values)
+    )(jnp.asarray(place_table()), batch_blocks.T, live_count, point_weights, basis_values)
 
 
 MESH = pl.DeviceIdType.MESH
-X_FIRST = (True, False, True, False, True, False)
-
-
-def exchange_kernel(mask, partial, out, relay, direct, final, stage, relay2, direct2, final2, half_sum,
-                    send, send_half, sem1, sem2, send1, send2, arrive, leave):
+
+def exchange_kernel(mask, partial, out, relay, direct, final, stage, relay2, direct2, final2,
+                    send, send_half, pass_by, sem1, sem2, send1, send2, arrive, leave, passing, sweeps):
     dom, grp = lax.axis_index("dom"), lax.axis_index("grp")
     x, z = grp % 4, grp // 4
 
     def at(first, second, x_first):
         return second * 4 + first if x_first else first * 4 + second
 
+    x_near = [(dom, at((x + n) % 4, z, True)) for n in (1, 3)]
+    z_near = [(dom, at(x, (z + n) % 4, True)) for n in (1, 3)]
+    y_near = [((dom + n) % 8, grp) for n in (2, 6)]
+    core_near = [(dom // 2 * 2 + 1 - dom % 2, grp)]
+
+    def signal(sem, peers):
+        for peer in peers:
+            pl.semaphore_signal(sem, inc=1, device_id=peer, device_id_type=MESH)
+
     barrier = pltpu.get_barrier_semaphore()
-    peers = [(dom, z * 4 + (x + 1) % 4), (dom, z * 4 + (x + 3) % 4),
-             (dom, (z + 1) % 4 * 4 + x), (dom, (z + 3) % 4 * 4 + x)]
-    peers += [((dom + n) % 8, grp) for n in range(1, 8)]
-    source = (grp + 1 + (dom - grp - 1) % 8) % 16
-    peers += [(n, source) for n in range(8)]
-    for peer in peers:
-        pl.semaphore_signal(barrier, inc=1, device_id=peer, device_id_type=MESH)
-    pl.semaphore_wait(barrier, len(peers))
+    everyone = x_near + z_near + y_near + core_near
+    signal(barrier, everyone)
+    pl.semaphore_wait(barrier, len(everyone))
+    todo = [x_near, z_near, z_near, y_near, y_near, core_near]
+
+    def sweep():
+        if todo:
+            n = 6 - len(todo)
+            peers = todo.pop(0)
+            signal(sweeps.at[n], peers)
+            pl.semaphore_wait(sweeps.at[n], len(peers))
 
     def piece(k, owner, h):
-        if k < 4:
-            return partial.at[pl.ds(64 * k + 4 * owner + 2 * h, 2)]
-        return partial.at[pl.ds(256 + owner, 1), pl.ds((k - 4) * 32 + 16 * h, 16), :]
+        return partial.at[pl.ds(BASES[k] + sum(SIZES[k]) * owner + h * SIZES[k][0], SIZES[k][h])]
 
     def view(buffers, k, *index):
-        return buffers[k // 4].at[(k % 4, *index)]
+        return buffers[k].at[(*index, pl.ds(0, SIZES[k][index[-1]]))]
 
     def remote(src, dst, send_sem, recv_sem, peer):
         return pltpu.make_async_remote_copy(src_ref=src, dst_ref=dst, send_sem=send_sem, recv_sem=recv_sem,
@@ -200,51 +236,38 @@
         return copy
 
     ORDER = (2, 1, 3, 0)
-
-    def begin(ks):
-        for s in ORDER:
-            for k in ks:
+    items = [(r, s) for r in range(len(ROUNDS)) for s in ORDER]
+
+    def begin(r, s):
+        for kinds in ((0, 1), (2, 3)):
+            for k in ROUNDS[r]:
                 c, _ = copies1(k, s)
-                c(0).start()
-                c(1).start()
-        for s in ORDER:
-            for k in ks:
-                c, _ = copies1(k, s)
-                c(2).start()
-                c(3).start()
-
-    def pass_on(ks):
-        for s in ORDER:
-            for k in ks:
-                c, (right, left, mf, so, xf) = copies1(k, s)
-                for h, owner in ((0, right), (1, left)):
-                    c(h).wait_recv()
-                    slot = view(relay, k, s, h)
-                    slot[...] = slot[...] + piece(k, at(owner, so, xf), h)[...]
-                    c(4 + h).start()
-
-    def settle(ks):
-        for s in ORDER:
-            for k in ks:
-                c, (right, left, mf, so, xf) = copies1(k, s)
-                for h in (0, 1):
-                    c(4 + h).wait_recv()
-                    c(3 - h).wait_recv()
-                    view(stage, k, s, h)[...] = (
-                        piece(k, at(mf, so, xf), h)[...] + view(final, k, s, h)[...] + view(direct, k, s, h)[...]
-                    )
-            for k in ks:
-                c = copies2(k)
-                if s == 2:
-                    c(0).start()
-                    c(1).start()
-                if s == 1:
-                    c(2).start()
-                if s == 3:
-                    c(3).start()
-
-    def pass_on2(ks):
-        for k in ks:
+                for n in kinds:
+                    c(n).start()
+
+    def pass_on(r, s):
+        for k in ROUNDS[r]:
+            c, (right, left, mf, so, xf) = copies1(k, s)
+            for h, owner in ((0, right), (1, left)):
+                c(h).wait_recv()
+                slot = view(relay, k, s, h)
+                slot[...] = slot[...] + piece(k, at(owner, so, xf), h)[...]
+                c(4 + h).start()
+
+    def settle(r, s):
+        for k in ROUNDS[r]:
+            c, (right, left, mf, so, xf) = copies1(k, s)
+            for h in (0, 1):
+                c(4 + h).wait_recv()
+                c(3 - h).wait_recv()
+                view(stage, k, s, h)[...] = (
+                    piece(k, at(mf, so, xf), h)[...] + view(final, k, s, h)[...] + view(direct, k, s, h)[...]
+                )
+            for n in {2: (0, 1), 1: (2,), 3: (3,), 0: ()}[s]:
+                copies2(k)(n).start()
+
+    def pass_on2(r):
+        for k in ROUNDS[r]:
             c = copies2(k)
             for h, s in ((0, 1), (1, 3)):
                 c(h).wait_recv()
@@ -252,17 +275,21 @@
                 slot[...] = slot[...] + view(stage, k, s, h)[...]
                 c(4 + h).start()
 
-    def settle2(ks):
-        for k in ks:
+    def settle2(r):
+        for k in ROUNDS[r]:
             c = copies2(k)
             for h in (0, 1):
                 c(4 + h).wait_recv()
                 c(3 - h).wait_recv()
                 value = view(stage, k, 0, h)[...] + view(final2, k, h)[...] + view(direct2, k, h)[...]
-                if k < 4:
-                    hand_out(2 * k + h, value.reshape(128, 128))
-                else:
-                    half_sum[(k - 4) * 32 + 16 * h : (k - 4) * 32 + 16 * h + 16, :] = value[0]
+                ahead = 0
+                for q in SLABS[k][1 + h]:
+                    if q == 8:
+                        hand_out_half(value[ahead])
+                        ahead += 1
+                    else:
+                        hand_out(q, value[ahead : ahead + 2].reshape(128, 128))
+                        ahead += 2
 
     lane = lax.broadcasted_iota(jnp.int32, (64, 128), 1)
     low_half = lax.broadcasted_iota(jnp.int32, (128, 128), 1) < 64
@@ -288,8 +315,28 @@
             pltpu.make_async_copy(src, dst, arrive.at[dom, a // 8]).start()
 
     def to_other(src, a, rows, n):
-        dst = out.at[dom, grp // 8, rows]
-        return remote(src, dst, leave.at[1, n], arrive.at[dom, grp // 8], (grp % 8, a))
+        return remote(src, pass_by.at[n, rows], leave.at[1, n], passing.at[n], (dom, a))
+
+    def forward(n):
+        g = (grp + n) % 16
+        rows = pl.ds(pl.multiple_of(g // 8 * 64, 64), 64) if n == 8 else whole
+        to_other(pass_by.at[n, rows], g, rows, n).wait_recv()
+        target = g % 8
+        src, dst = pass_by.at[n, rows], out.at[dom, g // 8, rows]
+
+        @pl.when(target != dom)
+        def _():
+            remote(src, dst, leave.at[2, n], arrive.at[dom, g // 8], (target, grp)).start()
+
+        @pl.when(target == dom)
+        def _():
+            pltpu.make_async_copy(src, dst, arrive.at[dom, g // 8]).start()
+
+    def forward_round(r):
+        for k in ROUNDS[r]:
+            for q in SLABS[k][1] + SLABS[k][2]:
+                if q:
+                    forward(q)
 
     whole = pl.ds(0, 128)
 
@@ -306,11 +353,10 @@
         send[1, n] = jnp.where(wrapped, value, turned) * kept(grp, a)
         to_other(send.at[1, n], a, whole, n).start()
 
-    def hand_out_half():
+    def hand_out_half(value):
         a = (grp + 8) % 16
         h = grp // 8
         low, high = grp % 8, grp % 8 + 8
-        value = half_sum[...]
         upper = value * jnp.where(lane < 64, factor(low + 16 * h, high), factor(low + 16 * h, high + 16))
         lower = value * jnp.where(lane < 64, factor(high, low + 16 * h), factor(high + 16, low + 16 * h))
         rows = pl.ds(pl.multiple_of(h * 64, 64), 64)
@@ -319,20 +365,27 @@
         send_half[1] = jnp.where(h == 0, upper, lower)
         to_other(send_half.at[1], a, rows, 8).start()
 
-    first, last = (0, 1), (4, 5, 2, 3)
-    begin(first)
-    pass_on(first)
-    begin(last)
-    settle(first)
-    pass_on(last)
-    pass_on2(first)
-    settle2(first)
-    settle(last)
-    pass_on2(last)
-    settle2(last)
-    hand_out_half()
-
-    for k in range(6):
+    begin(*items[0])
+    for i, (r, s) in enumerate(items):
+        if i + 1 < len(items):
+            begin(*items[i + 1])
+        pass_on(r, s)
+        if i:
+            settle(*items[i - 1])
+        sweep()
+        if r and s == 2:
+            pass_on2(r - 1)
+        if r and s == 3:
+            settle2(r - 1)
+        if r > 1 and s == 2:
+            forward_round(r - 2)
+    settle(*items[-1])
+    pass_on2(len(ROUNDS) - 1)
+    forward_round(len(ROUNDS) - 2)
+    settle2(len(ROUNDS) - 1)
+    forward_round(len(ROUNDS) - 1)
+
+    for k in range(len(SLABS)):
         for s in range(4):
             for n in range(6):
                 copies1(k, s)[0](n).wait_send()
@@ -349,32 +402,41 @@
 
         if n:
             to_other(src.at[1], a, rows, n).wait_send()
+            g = (grp + n) % 16
+
+            @pl.when(g % 8 != dom)
+            def _():
+                remote(src.at[1], out.at[dom, g // 8, rows], leave.at[2, n], arrive.at[dom, g // 8],
+                       (g % 8, grp)).wait_send()
     for d in range(8):
         for t in range(2):
             pltpu.make_async_copy(out.at[d, t], out.at[d, t], arrive.at[d, t]).wait()
 
 
 def exchange(partial, pair_mask):
-    def pair(*lead):
-        return [pltpu.VMEM((4, *lead, 2, 64, 128), jnp.float32), pltpu.VMEM((2, *lead, 1, 16, 128), jnp.float32)]
-
-    buffers = [pair(4, 2), pair(4, 2), pair(4, 2), pair(4, 2), pair(2), pair(2), pair(2)]
-    flat = [b for two in buffers for b in two]
+    count = len(SLABS)
+
+    def per_slab(*lead):
+        return [pltpu.VMEM((*lead, max(n), 64, 128), jnp.float32) for n in SIZES]
+
+    flat = [b for lead in ((4, 2),) * 4 + ((2,),) * 3 for b in per_slab(*lead)]
     rest = [
-        pltpu.VMEM((64, 128), jnp.float32),
         pltpu.VMEM((2, 8, 128, 128), jnp.float32),
         pltpu.VMEM((2, 64, 128), jnp.float32),
-        pltpu.SemaphoreType.DMA((6, 4, 6)),
-        pltpu.SemaphoreType.DMA((6, 6)),
-        pltpu.SemaphoreType.DMA((6, 4, 6)),
-        pltpu.SemaphoreType.DMA((6, 6)),
+        pltpu.VMEM((9, 128, 128), jnp.float32),
+        pltpu.SemaphoreType.DMA((count, 4, 6)),
+        pltpu.SemaphoreType.DMA((count, 6)),
+        pltpu.SemaphoreType.DMA((count, 4, 6)),
+        pltpu.SemaphoreType.DMA((count, 6)),
         pltpu.SemaphoreType.DMA((8, 2)),
-        pltpu.SemaphoreType.DMA((2, 9)),
+        pltpu.SemaphoreType.DMA((3, 9)),
+        pltpu.SemaphoreType.DMA((9,)),
+        pltpu.SemaphoreType.REGULAR((6,)),
     ]
 
     def body(mask, partial, out, *refs):
-        pairs = [refs[2 * n : 2 * n + 2] for n in range(7)]
-        exchange_kernel(mask, partial, out, *pairs, *refs[14:])
+        groups = [refs[count * n : count * n + count] for n in range(7)]
+        exchange_kernel(mask, partial, out, *groups, *refs[7 * count :])
 
     return pl.pallas_call(
         body,
@@ -383,7 +445,7 @@
         out_specs=pl.BlockSpec(memory_space=pl.ANY),
         scratch_shapes=flat + rest,
         compiler_params=pltpu.CompilerParams(
-            collective_id=0, has_side_effects=True, vmem_limit_bytes=48 * 2**20
+            collective_id=0, has_side_effects=True, vmem_limit_bytes=26 * 2**20
         ),
         name="exchange",
     )(pair_mask, partial)

time: 128 us -> 104 us (0.81)
  the two profiles are of different devices: /device:TPU:1 before, /device:TPU:41 now
where the time goes in v2:
time: 104 us; the launch traced here: 103 us
  Pallas kernels  100 us (96%)
  local copies, waits for them, and re-layouts  2.27 us (2%)
    pallas_call x1, Pallas kernels, exchange(): pl.pallas_call(body, out_shape=jax.ShapeDtypeStruct((8, 2, 128, 128), jnp...  78.9 us
    pallas_call x1, Pallas kernels, products(): pl.pallas_call(products_kernel, out_shape=jax.ShapeDtypeStruct((TILES, 64...  15.3 us
    pallas_call x1, Pallas kernels, place(): pl.pallas_call(place_kernel, out_shape=jax.ShapeDtypeStruct((2048, 1024),...  6.06 us
    unnamed x10, local copies, waits for them, and re-layouts  2.27 us

profile of v2, /device:TPU:41, one launch (start us, length us, event | category | flops | bytes accessed | tf_op | source)
XLA Modules:
  0.0 103.3 jit_solution(4752030463858987079)
XLA Ops:
  0.7 0.0 copy-start
  0.7 0.9 copy-done
  1.6 0.0 copy-start.2
  1.6 0.7 copy-done.2
  2.2 0.0 copy-start.4
  2.2 0.7 copy-done.4
  2.9 0.0 copy-start.1
  2.9 15.3 %products.1.partial = f32[272,64,128]{2,1,0:T(8,128)S(1)} custom-call(s32[512]{0:T(512)S(1)} %copy-done.4, s32[5,112]{1,0:T(8,128)S(1)} %bitcast.1, s32[1,1]{1,0:T(1,128)S(6)} %copy.8.live, f32[112,256]{1,0:T(8,128)S(1)} %copy-done, bf16[112,320,256]{2,1,0:T(8,128)(2,1)} %basis.1), custom_call_target="tpu_custom_call" | custom-call | tf_op jit(solution)/shard_map/products/pallas_call | solution.py:134
  18.3 0.0 copy-done.1
  18.3 0.0 copy-start.3
  18.3 78.9 %exchange.1.tiles = f32[8,2,128,128]{3,2,1,0:T(8,128)S(1)} custom-call(s32[1,32,32]{2,1,0:T(8,128)S(1)} %copy-done.1, f32[272,64,128]{2,1,0:T(8,128)S(1)} %products.1.partial), custom_call_target="tpu_custom_call" | custom-call | tf_op jit(solution)/shard_map/exchange/pallas_call | solution.py:441
  97.2 0.0 copy-done.3
  97.3 6.1 %place.1 = f32[2048,1024]{1,0:T(8,128)} custom-call(s32[8,32]{1,0:T(8,128)S(1)} %copy-done.3, f32[8,2,128,128]{3,2,1,0:T(8,128)S(1)} %exchange.1.tiles), custom_call_target="tpu_custom_call" | custom-call | tf_op jit(solution)/shard_map/place/pallas_call | solution.py:488
Async XLA Ops:
  0.7 0.9 copy-start
  1.6 0.7 copy-start.2
  2.2 0.7 copy-start.4
  2.9 15.4 %copy-start.1 = (s32[1,32,32]{2,1,0:T(8,128)S(1)}, s32[1,32,32]{2,1,0:T(8,128)}, u32[]{:S(2)}) copy-start(s32[1,32,32]{2,1,0:T(8,128)} %mask.1) | copy-start | bytes 12292
  18.3 79.0 %copy-start.3 = (s32[8,32]{1,0:T(8,128)S(1)}, s32[8,32]{1,0:T(8,128)}, u32[]{:S(2)}) copy-start(s32[8,32]{1,0:T(8,128)} %ids.1) | copy-start | bytes 3076
